TPU v7x, 256 devices: a whole 4x4x8 slice. The times are simulated.
256 devices in a mesh: rows: 8 (over y, core), labels: 32 (over x, z).
Axes of the slice: x: 4, y: 4, z: 8, core: 2. Of those that a mesh axis runs over, the one named last changes fastest.
Arguments:
- embeddings: bfloat16 [8192, 768], P(('rows', 'labels')), may hold values from -6 to 6
- class_weight: bfloat16 [65536, 768], P('labels'), may hold values from -0.4375 to 0.4375
- class_bias: float32 [65536], P('labels'), may hold values from -10 to -8
- propensity: float32 [65536], P('labels'), may hold values from 0.1 to 0.9
- label_ids: int32 [8192, 32], P('rows'), may hold values from 0 to 65535
- label_count: int32 [8192], P('rows'), may hold values from 1 to 32
- label_bins: int32 [65536], P('labels'), may hold values from 0 to 15
- prior_mean: float32 [16], replicated, may hold values from 0.1 to 0.9
Outputs:
- new_propensity: float32 [65536], P('labels')
- weight_grad: bfloat16 [65536, 768], P('labels', 'rows')
- embed_grad: bfloat16 [8192, 768], P(('rows', 'labels'))
Inputs may be any that keep to these rules, and one draw needn't show every extreme that they name: `label_ids`: entries past a row's count are padding and are ignored; ids may repeat.
All inputs are finite; a program needn't handle non-finite values.
Results may differ from a plain program's by a relative error of at most 0.014.
Values may be sent and summed in bfloat16 or wider, within the bound.
No kernel may reach another device: no remote copies, remote signals or barrier semaphores. Data moves between devices by JAX's collectives and lax.ppermute only.
A program may use at most 64 MiB of HBM per device.

v0:
```python
import jax
import jax.numpy as jnp
from jax import lax
from jax.sharding import PartitionSpec as P


def dense_observed(label_ids, label_count, offset, width):
    slots = jnp.arange(label_ids.shape[1], dtype=jnp.int32)
    local = label_ids - offset
    valid = (slots[None, :] < label_count[:, None]) & (local >= 0) & (local < width)
    column = jnp.where(valid, local, width)
    lanes = jnp.arange(width, dtype=jnp.int32)
    hits = column[:, :, None] == lanes[None, None, :]
    return jnp.max(hits.astype(jnp.float32), axis=1)


def bin_prior(bins, prior_mean):
    levels = jnp.arange(prior_mean.shape[0], dtype=jnp.int32)
    onehot = (bins[:, None] == levels[None, :]).astype(jnp.float32)
    return jnp.sum(onehot * prior_mean[None, :], axis=1)


def body(
    embeddings, class_weight, class_bias, propensity, label_ids, label_count, label_bins, prior_mean
):
    width = class_weight.shape[0]
    gathered = lax.all_gather(embeddings, "labels", axis=0, tiled=True)
    offset = lax.axis_index("labels") * width
    scores = (
        lax.dot_general(
            gathered, class_weight, (((1,), (1,)), ((), ())), preferred_element_type=jnp.float32
        )
        + class_bias[None, :]
    )
    prob = jax.nn.sigmoid(scores)
    observed = dense_observed(label_ids, label_count, offset, width)
    posterior = observed + (1.0 - observed) * prob * (1.0 - propensity[None, :]) / (
        1.0 - prob * propensity[None, :]
    )
    local_post = jnp.sum(posterior, axis=0)
    local_obs = jnp.sum(observed, axis=0)
    post_sum, obs_sum = lax.psum((local_post, local_obs), "rows")
    updated = (obs_sum + 8.0 * bin_prior(label_bins, prior_mean)) / (post_sum + 8.0)
    residual_grad = (prob - posterior).astype(jnp.bfloat16)
    weight_terms = lax.dot_general(
        residual_grad, gathered, (((0,), (0,)), ((), ())), preferred_element_type=jnp.float32
    )
    weight_summed = lax.psum_scatter(
        weight_terms.astype(jnp.bfloat16), "rows", scatter_dimension=1, tiled=True
    ).astype(jnp.float32)
    weight_grad = (weight_summed / updated[:, None]).astype(jnp.bfloat16)
    scaled_weight = (class_weight.astype(jnp.float32) / updated[:, None]).astype(jnp.bfloat16)
    embed_terms = jnp.dot(residual_grad, scaled_weight, preferred_element_type=jnp.float32)
    embed_total = lax.psum_scatter(
        embed_terms.astype(jnp.bfloat16), "labels", scatter_dimension=0, tiled=True
    )
    return (updated, weight_grad, embed_total)


def solution(mesh):
    placed = (
        P(("rows", "labels"), None),
        P("labels", None),
        P("labels"),
        P("labels"),
        P("rows", None),
        P("rows"),
        P("labels"),
        P(),
    )
    return jax.shard_map(
        body,
        mesh=mesh,
        in_specs=placed,
        out_specs=(P("labels"), P("labels", "rows"), P(("rows", "labels"), None)),
        check_vma=False,
    )
```

profile of v0, /device:TPU:16, one launch (start us, length us, event | category | flops | bytes accessed | tf_op | source)
XLA Modules:
  0.0 372.5 jit_solution(14143030236094921360)
XLA Ops:
  7.2 0.0 copy-start.1
  7.2 0.0 copy-start.6
  7.2 0.0 all-gather.2.cloned.1.call-start
  7.2 0.7 all-gather.2.cloned.1.call-update
  7.9 0.0 reduce-scatter.3.cloned.1.call-start
  8.0 0.9 fusion.5
  8.9 0.2 copy.12
  9.1 0.7 broadcast_subtract_fusion
  9.8 51.6 %convert_reduce_fusion = f32[1024,2048]{1,0:T(8,128)} fusion(s32[1024,32]{1,0:T(8,128)S(1)} %copy.12), kind=kLoop, calls=%fused_computation | loop fusion | flops 199229440 | bytes 8519680 | tf_op jit(solution)/shard_map/reduce_max | solution.py:14
  61.5 28.8 %all-gather.2.cloned.1.call-done = bf16[1024,768]{1,0:T(8,128)(2,1)} async-done(((bf16[32,768]{1,0:T(8,128)(2,1)}), bf16[1024,768]{1,0:T(8,128)(2,1)}) %all-gather.2.cloned.1.call-update) | async-done | bytes 1572880 | tf_op jit(solution)/shard_map/all_gather | solution.py:27
  90.3 0.0 copy-done.1
  90.3 0.0 copy-done.6
  90.3 10.4 %fusion.6 = (f32[2048]{0:T(1024)S(1)}, f32[2048]{0:T(1024)S(1)}, bf16[1024,2048]{1,0:T(8,128)(2,1)S(1)}) fusion(f32[1024,2048]{1,0:T(8,128)} %convert_reduce_fusion, f32[2048]{0:T(1024)S(1)} %copy-done.1, f32[2048]{0:T(1024)S(1)} %broadcast_subtract_fusion, f32[2048]{0:T(1024)S(1)} %copy-done.6, bf16[1024,768]{1,0:T(8,128)(2,1)} %all-gather.2.cloned.1.call-done, ...), kind=kOutput, calls=%fused_computation.19 | convolution fusion | flops 3252678656 | bytes 17342464 | tf_op jit(solution)/shard_map/dot_general | solution.py:30
  100.7 0.0 copy-start.7
  100.7 1.9 copy-done.7
  102.6 0.0 copy-done.5
  102.6 0.0 copy-start.2
  102.7 5.0 %convolution_convert_fusion = bf16[2048,768]{0,1:T(8,128)(2,1)} fusion(bf16[1024,2048]{1,0:T(8,128)(2,1)S(1)} %get-tuple-element.7, bf16[1024,768]{1,0:T(8,128)(2,1)S(1)} %copy-done.5), kind=kOutput, calls=%fused_computation.6 | convolution fusion | flops 3222798336 | bytes 8912896 | tf_op jit(solution)/shard_map/dot_general | solution.py:45
  107.7 0.0 reduce-scatter.3.cloned.1.call-update
  107.7 0.0 reduce-scatter.5.cloned.1.call-start
  107.8 0.0 copy-done.2
  107.8 0.0 copy-done.3
  107.8 0.1 select_reduce_fusion
  107.9 19.3 %all-reduce = (f32[2048]{0:T(1024)S(1)}, f32[2048]{0:T(1024)S(1)}) all-reduce(f32[2048]{0:T(1024)S(1)} %get-tuple-element.4, f32[2048]{0:T(1024)S(1)} %get-tuple-element.3), channel_id=1, replica_groups=mesh['rows'=8,'labels'=32] {'rows'}, use_global_device_ids=true, to_apply=%region_5.6 | all-reduce | flops 4096 | bytes 32768 | tf_op jit(solution)/shard_map/psum | solution.py:42
  127.2 0.0 copy-done.4
  127.2 0.0 copy-start
  127.3 7.0 %fusion.1 = bf16[1024,768]{1,0:T(8,128)(2,1)} fusion(bf16[1024,2048]{1,0:T(8,128)(2,1)} %copy-done.7, bf16[2048,768]{1,0:T(8,128)(2,1)S(1)} %copy-done.4, f32[2048]{0:T(1024)S(1)} %add_divide_fusion.1), kind=kOutput, calls=%fused_computation.8 | convolution fusion | flops 3226730496 | bytes 8921088 | tf_op jit(solution)/shard_map/dot_general | solution.py:53
  134.3 0.0 reduce-scatter.5.cloned.1.call-update
  134.3 4.8 %reduce-scatter.3.cloned.1.call-done = bf16[2048,96]{0,1:T(8,128)(2,1)} async-done(((bf16[2048,768]{0,1:T(8,128)(2,1)}), bf16[2048,96]{0,1:T(8,128)(2,1)}) %reduce-scatter.3.cloned.1.call-update) | async-done | bytes 393232 | tf_op jit(solution)/shard_map/reduce_scatter | solution.py:48
  139.1 0.0 copy-done
  139.1 1.8 divide_convert_fusion.4
  140.9 225.0 %reduce-scatter.5.cloned.1.call-done = bf16[32,768]{1,0:T(8,128)(2,1)} async-done(((bf16[1024,768]{1,0:T(8,128)(2,1)}), bf16[32,768]{1,0:T(8,128)(2,1)}) %reduce-scatter.5.cloned.1.call-update) | async-done | bytes 49168 | tf_op jit(solution)/shard_map/reduce_scatter | solution.py:54
  (4 shorter events, 0.0 us)
Async XLA Ops:
  7.2 83.1 %copy-start.1 = (f32[2048]{0:T(1024)S(1)}, f32[2048]{0:T(1024)}, u32[]{:S(2)}) copy-start(f32[2048]{0:T(1024)} %param.11) | copy-start | bytes 24580
  7.2 83.1 %copy-start.6 = (f32[2048]{0:T(1024)S(1)}, f32[2048]{0:T(1024)}, u32[]{:S(2)}) copy-start(f32[2048]{0:T(1024)} %param.10) | copy-start | bytes 24580
  7.2 83.1 %all-gather.2.cloned.1.call-start = ((), (), s32[]{:S(2)}) async-start(), calls=%async_computation.2 | async-start | bytes 1622016 | tf_op jit(solution)/shard_map/all_gather | solution.py:27
  7.9 131.2 %reduce-scatter.3.cloned.1.call-start = ((), (), s32[]{:S(2)}) async-start(), calls=%async_computation.3 | async-start | bytes 3538944 | tf_op jit(solution)/shard_map/reduce_scatter | solution.py:48
  90.3 12.3 %copy-start.5 = (bf16[1024,768]{1,0:T(8,128)(2,1)S(1)}, bf16[1024,768]{1,0:T(8,128)(2,1)}, u32[]{:S(2)}) copy-start(bf16[1024,768]{1,0:T(8,128)(2,1)} %all-gather.2.cloned.1.call-done) | copy-start | bytes 4718596
  100.7 1.9 copy-start.7
  102.6 5.1 %copy-start.2 = (s32[2048]{0:T(1024)S(1)}, s32[2048]{0:T(1024)}, u32[]{:S(2)}) copy-start(s32[2048]{0:T(1024)} %param.14) | copy-start | bytes 24580
  102.6 5.1 %copy-start.3 = (f32[16]{0:T(128)S(1)}, f32[16]{0:T(128)}, u32[]{:S(2)}) copy-start(f32[16]{0:T(128)} %param.15) | copy-start | bytes 196
  102.6 24.6 %copy-start.4 = (bf16[2048,768]{1,0:T(8,128)(2,1)S(1)}, bf16[2048,768]{1,0:T(8,128)(2,1)}, u32[]{:S(2)}) copy-start(bf16[2048,768]{1,0:T(8,128)(2,1)} %param.9) | copy-start | bytes 9437188
  107.7 258.2 %reduce-scatter.5.cloned.1.call-start = ((), (), s32[]{:S(2)}) async-start(), calls=%async_computation.4 | async-start | bytes 1622016 | tf_op jit(solution)/shard_map/reduce_scatter | solution.py:54
  127.2 11.9 %copy-start = (f32[2048]{0:T(1024)}, f32[2048]{0:T(1024)S(1)}, u32[]{:S(2)}) copy-start(f32[2048]{0:T(1024)S(1)} %add_divide_fusion.1) | copy-start | bytes 24580
Sparse Core Ops, SparseCore 0:
  10.6 79.6 all-gather.1
  107.8 31.2 reduce-scatter.2
  143.5 222.3 reduce-scatter.4
where the time goes:
time: 373 us; the launch traced here: 372 us
  waiting for transfers between devices  259 us (69%)
  other arithmetic  55.2 us (15%)
  matrix products  22.4 us (6%)
  blocking collectives  19.3 us (5%)
  between operations  13.8 us (4%)
    reduce_scatter x1, waiting for transfers between devices, body(): lax.psum_scatter(embed_terms.astype(jnp.bfloat16), 'labels', scatter_dime...  225 us
    reduce_max x1, other arithmetic, dense_observed(): return jnp.max(hits.astype(jnp.float32), axis=1)  51.6 us
    all_gather x1, waiting for transfers between devices, body(): gathered = lax.all_gather(embeddings, 'labels', axis=0, tiled=True)  28.8 us
    psum x1, blocking collectives, body(): post_sum, obs_sum = lax.psum((local_post, local_obs), 'rows')  19.3 us
    dot_general x1, matrix products, body(): lax.dot_general(gathered, class_weight, (((1,), (1,)), ((), ())), preferr...  10.4 us
  transfers between devices with their start and end apart: 3, of which 3 were waited for; matrix products, arithmetic and copies ran while one was open for 17% of the time, Pallas kernels for 0%

commit v1 on v0

--- a/solution.py
+++ b/solution.py
@@ -24,7 +24,9 @@
     embeddings, class_weight, class_bias, propensity, label_ids, label_count, label_bins, prior_mean
 ):
     width = class_weight.shape[0]
-    gathered = lax.all_gather(embeddings, "labels", axis=0, tiled=True)
+    gathered = jnp.concatenate(
+        lax.all_to_all(jnp.stack([embeddings] * lax.axis_size("labels")), "labels", 0, 0), axis=0
+    )
     offset = lax.axis_index("labels") * width
     scores = (
         lax.dot_general(

time: 373 us -> 361 us (0.968)
  waiting for transfers between devices: 259 us -> 232 us
  starting transfers between devices: 0.12 us -> 11.5 us
    all_gather x1 -> x0, waiting for transfers between devices: 28.8 us -> none  [body(): gathered = lax.all_gather(embeddings, 'labels', axis=0, tiled=True)]
    all_to_all x0 -> x1, starting transfers between devices: none -> 11.4 us  [body(): lax.all_to_all(jnp.stack([embeddings] * lax.axis_size('labels')), 'labels...]
  transfers between devices with their start and end apart: 3 -> 3, of which waited for: 3 -> 2; matrix products, arithmetic and copies ran while one was open for 17% -> 18% of each run, Pallas kernels for 0% -> 0%
where the time goes in v1:
time: 361 us; the launch traced here: 360 us
  waiting for transfers between devices  232 us (64%)
  other arithmetic  55.2 us (15%)
  matrix products  23.2 us (6%)
  blocking collectives  19.7 us (5%)
  between operations  14.1 us (4%)
  starting transfers between devices  11.5 us (3%)
  local copies, waits for them, and re-layouts  4.35 us (1%)
    reduce_scatter x1, waiting for transfers between devices, body(): lax.psum_scatter(embed_terms.astype(jnp.bfloat16), 'labels', scatter_dime...  225 us
    reduce_max x1, other arithmetic, dense_observed(): return jnp.max(hits.astype(jnp.float32), axis=1)  51.6 us
    psum x1, blocking collectives, body(): post_sum, obs_sum = lax.psum((local_post, local_obs), 'rows')  19.7 us
    all_to_all x1, starting transfers between devices, body(): lax.all_to_all(jnp.stack([embeddings] * lax.axis_size('labels')), 'labels...  11.4 us
    dot_general x1, matrix products, body(): lax.dot_general(gathered, class_weight, (((1,), (1,)), ((), ())), preferr...  10.1 us
    dot_general x1, matrix products, body(): jnp.dot(residual_grad, scaled_weight, preferred_element_type=jnp.float32)  8.08 us
  transfers between devices with their start and end apart: 3, of which 2 were waited for; matrix products, arithmetic and copies ran while one was open for 18% of the time, Pallas kernels for 0%

profile of v1, /device:TPU:16, one launch (start us, length us, event | category | flops | bytes accessed | tf_op | source)
XLA Modules:
  0.0 360.3 jit_solution(7804694392445038440)
XLA Ops:
  7.2 2.2 stack.2
  9.4 0.0 copy-start.1
  9.4 0.0 copy-start.4
  9.4 11.4 %all-to-all-start = ((bf16[32,32,768]{2,1,0:T(8,128)(2,1)}), bf16[32,32,768]{2,1,0:T(8,128)(2,1)S(1)}, u32[]{:S(2)}, u32[]{:S(2)}) async-start(bf16[32,32,768]{2,1,0:T(8,128)(2,1)} %stack.2), calls=%async_computation | async-start | bytes 3145728 | tf_op jit(solution)/shard_map/all_to_all | solution.py:28
  20.8 0.0 reduce-scatter.3.cloned.1.call-start
  20.9 0.9 fusion.5
  21.8 0.2 copy.12
  22.0 0.7 broadcast_subtract_fusion
  22.7 51.6 %convert_reduce_fusion = f32[1024,2048]{1,0:T(8,128)} fusion(s32[1024,32]{1,0:T(8,128)S(1)} %copy.12), kind=kLoop, calls=%fused_computation | loop fusion | flops 199229440 | bytes 8519680 | tf_op jit(solution)/shard_map/reduce_max | solution.py:14
  74.4 0.0 all-to-all-done
  74.4 0.0 copy-done.1
  74.4 0.0 copy-done.4
  74.4 10.1 %fusion.6 = (f32[2048]{0:T(1024)S(1)}, f32[2048]{0:T(1024)S(1)}, bf16[1024,2048]{1,0:T(8,128)(2,1)S(1)}) fusion(f32[1024,2048]{1,0:T(8,128)} %convert_reduce_fusion, f32[2048]{0:T(1024)S(1)} %copy-done.1, f32[2048]{0:T(1024)S(1)} %broadcast_subtract_fusion, f32[2048]{0:T(1024)S(1)} %copy-done.4, bf16[1024,768]{1,0:T(8,128)(2,1)S(1)} %bitcast.6, ...), kind=kOutput, calls=%fused_computation.19 | convolution fusion | flops 3252678656 | bytes 17342464 | tf_op jit(solution)/shard_map/dot_general | solution.py:32
  84.5 0.0 copy-start.5
  84.5 1.9 copy-done.5
  86.4 0.0 copy-start.2
  86.4 0.0 copy-start.3
  86.4 5.0 %convolution_convert_fusion = bf16[2048,768]{0,1:T(8,128)(2,1)} fusion(bf16[1024,2048]{1,0:T(8,128)(2,1)S(1)} %get-tuple-element.7, bf16[1024,768]{1,0:T(8,128)(2,1)S(1)} %bitcast.7), kind=kOutput, calls=%fused_computation.6 | convolution fusion | flops 3222798336 | bytes 8912896 | tf_op jit(solution)/shard_map/dot_general | solution.py:47
  91.5 0.0 reduce-scatter.3.cloned.1.call-update
  91.5 0.0 reduce-scatter.5.cloned.1.call-start
  91.5 0.0 copy-done.2
  91.5 0.0 copy-done.3
  91.6 0.1 select_reduce_fusion
  91.7 19.7 %all-reduce = (f32[2048]{0:T(1024)S(1)}, f32[2048]{0:T(1024)S(1)}) all-reduce(f32[2048]{0:T(1024)S(1)} %get-tuple-element.4, f32[2048]{0:T(1024)S(1)} %get-tuple-element.3), channel_id=1, replica_groups=mesh['rows'=8,'labels'=32] {'rows'}, use_global_device_ids=true, to_apply=%region_5.6 | all-reduce | flops 4096 | bytes 32768 | tf_op jit(solution)/shard_map/psum | solution.py:44
  111.4 0.0 copy-start
  111.4 8.1 %fusion.1 = bf16[1024,768]{1,0:T(8,128)(2,1)} fusion(bf16[1024,2048]{1,0:T(8,128)(2,1)} %copy-done.5, bf16[2048,768]{1,0:T(8,128)(2,1)} %param.9, f32[2048]{0:T(1024)S(1)} %add_divide_fusion.1), kind=kOutput, calls=%fused_computation.8 | convolution fusion | flops 3226730496 | bytes 8921088 | tf_op jit(solution)/shard_map/dot_general | solution.py:55
  119.4 0.0 reduce-scatter.5.cloned.1.call-update
  119.5 7.0 %reduce-scatter.3.cloned.1.call-done = bf16[2048,96]{0,1:T(8,128)(2,1)} async-done(((bf16[2048,768]{0,1:T(8,128)(2,1)}), bf16[2048,96]{0,1:T(8,128)(2,1)}) %reduce-scatter.3.cloned.1.call-update) | async-done | bytes 393232 | tf_op jit(solution)/shard_map/reduce_scatter | solution.py:50
  126.5 0.0 copy-done
  126.5 1.8 divide_convert_fusion.4
  128.3 225.1 %reduce-scatter.5.cloned.1.call-done = bf16[32,768]{1,0:T(8,128)(2,1)} async-done(((bf16[1024,768]{1,0:T(8,128)(2,1)}), bf16[32,768]{1,0:T(8,128)(2,1)}) %reduce-scatter.5.cloned.1.call-update) | async-done | bytes 49168 | tf_op jit(solution)/shard_map/reduce_scatter | solution.py:56
  (1 shorter events, 0.0 us)
Async XLA Ops:
  9.4 65.0 %copy-start.1 = (f32[2048]{0:T(1024)S(1)}, f32[2048]{0:T(1024)}, u32[]{:S(2)}) copy-start(f32[2048]{0:T(1024)} %param.11) | copy-start | bytes 24580
  9.4 65.0 %copy-start.4 = (f32[2048]{0:T(1024)S(1)}, f32[2048]{0:T(1024)}, u32[]{:S(2)}) copy-start(f32[2048]{0:T(1024)} %param.10) | copy-start | bytes 24580
  9.4 65.0 %all-to-all-start = ((bf16[32,32,768]{2,1,0:T(8,128)(2,1)}), bf16[32,32,768]{2,1,0:T(8,128)(2,1)S(1)}, u32[]{:S(2)}, u32[]{:S(2)}) async-start(bf16[32,32,768]{2,1,0:T(8,128)(2,1)} %stack.2), calls=%async_computation | async-start | bytes 3145728 | tf_op jit(solution)/shard_map/all_to_all | solution.py:28
  20.8 105.7 %reduce-scatter.3.cloned.1.call-start = ((), (), s32[]{:S(2)}) async-start(), calls=%async_computation.3 | async-start | bytes 3538944 | tf_op jit(solution)/shard_map/reduce_scatter | solution.py:50
  84.5 1.9 copy-start.5
  86.4 5.1 %copy-start.2 = (s32[2048]{0:T(1024)S(1)}, s32[2048]{0:T(1024)}, u32[]{:S(2)}) copy-start(s32[2048]{0:T(1024)} %param.14) | copy-start | bytes 24580
  86.4 5.1 %copy-start.3 = (f32[16]{0:T(128)S(1)}, f32[16]{0:T(128)}, u32[]{:S(2)}) copy-start(f32[16]{0:T(128)} %param.15) | copy-start | bytes 196
  91.5 262.0 %reduce-scatter.5.cloned.1.call-start = ((), (), s32[]{:S(2)}) async-start(), calls=%async_computation.4 | async-start | bytes 1622016 | tf_op jit(solution)/shard_map/reduce_scatter | solution.py:56
  111.4 15.2 %copy-start = (f32[2048]{0:T(1024)}, f32[2048]{0:T(1024)S(1)}, u32[]{:S(2)}) copy-start(f32[2048]{0:T(1024)S(1)} %add_divide_fusion.1) | copy-start | bytes 24580
Sparse Core Ops, SparseCore 0:
  91.6 34.8 reduce-scatter.2
  130.9 222.4 reduce-scatter.4
